TPU v7x, 32 devices: a whole 2x2x4 slice. The times are simulated.
32 devices in a mesh: fsdp: 8 (over y, x, core), seq: 4 (over z).
Axes of the slice: x: 2, y: 2, z: 4, core: 2. Of those that a mesh axis runs over, the one named last changes fastest.
Arguments:
- inputs: bfloat16 [8, 1568, 1024], P('fsdp', 'seq'), may hold values from -6 to 6
- clip_mask: int32 [8], P('fsdp'), may hold values 0 or 1
- ln1_gain: float32 [1024], replicated, may hold values from 0.5 to 1.5
- ln1_bias: float32 [1024], replicated, may hold values from -1 to 1
- w_query: bfloat16 [1024, 1024], P('fsdp'), may hold values from -0.1875 to 0.1875
- b_query: float32 [1024], replicated, may hold values from -1 to 1
- w_key: bfloat16 [1024, 1024], P('fsdp'), may hold values from -0.1875 to 0.1875
- w_value: bfloat16 [1024, 1024], P('fsdp'), may hold values from -0.1875 to 0.1875
- b_value: float32 [1024], replicated, may hold values from -1 to 1
- w_out: bfloat16 [1024, 1024], P('fsdp'), may hold values from -3 to 3
- b_out: float32 [1024], replicated, may hold values from -1 to 1
- ln2_gain: float32 [1024], replicated, may hold values from 0.5 to 1.5
- ln2_bias: float32 [1024], replicated, may hold values from -1 to 1
- w_fc1: bfloat16 [1024, 4096], P('fsdp'), may hold values from -0.1875 to 0.1875
- b_fc1: float32 [4096], replicated, may hold values from -1 to 1
- w_fc2: bfloat16 [4096, 1024], P('fsdp'), may hold values from -0.09375 to 0.09375
- b_fc2: float32 [1024], replicated, may hold values from -1 to 1
- cotangent: bfloat16 [8, 1568, 1024], P('fsdp', 'seq'), may hold values from -6 to 6
Outputs:
- output: bfloat16 [8, 1568, 1024], P('fsdp', 'seq')
- grad_inputs: float32 [8, 1568, 1024], P('fsdp', 'seq')
- grad_ln1_gain: float32 [1024], P(('fsdp', 'seq'))
- grad_ln1_bias: float32 [1024], P(('fsdp', 'seq'))
- grad_w_query: float32 [1024, 1024], P(('fsdp', 'seq'))
- grad_b_query: float32 [1024], P(('fsdp', 'seq'))
- grad_w_key: float32 [1024, 1024], P(('fsdp', 'seq'))
- grad_w_value: float32 [1024, 1024], P(('fsdp', 'seq'))
- grad_b_value: float32 [1024], P(('fsdp', 'seq'))
- grad_w_out: float32 [1024, 1024], P(('fsdp', 'seq'))
- grad_b_out: float32 [1024], P(('fsdp', 'seq'))
- grad_ln2_gain: float32 [1024], P(('fsdp', 'seq'))
- grad_ln2_bias: float32 [1024], P(('fsdp', 'seq'))
- grad_w_fc1: float32 [1024, 4096], P(('fsdp', 'seq'))
- grad_b_fc1: float32 [4096], P(('fsdp', 'seq'))
- grad_w_fc2: float32 [4096, 1024], P(('fsdp', 'seq'))
- grad_b_fc2: float32 [1024], P(('fsdp', 'seq'))
Inputs may be any that keep to these rules, and one draw needn't show every extreme that they name: `clip_mask`: 1 where the clip's slot holds a clip, 0 where it holds none.
All inputs are finite; a program needn't handle non-finite values. No bound on the sum of `clip_mask` on one device may be relied on, other than what follows from the above.
Results may differ from a plain program's by a relative error of at most 0.011.
Values may be sent and summed in bfloat16 or wider, within the bound.
No kernel may reach another device: no remote copies, remote signals or barrier semaphores. Data moves between devices by JAX's collectives and lax.ppermute only.
A program may use at most 256 MiB of HBM per device.

v0:
```python
import jax
import jax.numpy as jnp
from jax import lax
from jax.sharding import PartitionSpec as P

HEADS = 16
HD = 64
EPSILON = 1e-06


def normalize(rows, gain, shift):
    center = rows - jnp.mean(rows, -1, keepdims=True)
    inverse = lax.rsqrt(jnp.mean(center * center, -1, keepdims=True) + EPSILON)
    normed = center * inverse
    return (normed * gain + shift, normed, inverse)


def norm_grad(grad, normed, inverse, gain):
    scaled = grad * gain
    inner = (
        scaled
        - jnp.mean(scaled, -1, keepdims=True)
        - normed * jnp.mean(scaled * normed, -1, keepdims=True)
    )
    return inner * inverse


def to_pairs(array):
    clips, length, heads_here, size = array.shape
    return array.transpose(0, 2, 1, 3).reshape(clips * heads_here, length, size)


def from_pairs(array, clips):
    pairs, length, size = array.shape
    return array.reshape(clips, pairs // clips, length, size).transpose(0, 2, 1, 3)


def head_forward(blocks):
    query, keys, values = blocks
    scale = query.shape[-1] ** (-0.5)
    scores = jnp.dot(query, keys.T, preferred_element_type=jnp.float32) * scale
    peak = jnp.max(scores, -1, keepdims=True)
    expo = jnp.exp(scores - peak)
    total = jnp.sum(expo, -1, keepdims=True)
    weights = (expo / total).astype(jnp.bfloat16)
    mixed = jnp.dot(weights, values, preferred_element_type=jnp.float32).astype(jnp.bfloat16)
    return (mixed, (peak + jnp.log(total))[:, 0])


def head_backward(blocks):
    query, keys, values, grad_out, logsum = blocks
    scale = query.shape[-1] ** (-0.5)
    scores = jnp.dot(query, keys.T, preferred_element_type=jnp.float32) * scale
    probs = jnp.exp(scores - logsum[:, None])
    grad_probs = jnp.dot(grad_out, values.T, preferred_element_type=jnp.float32)
    inner = jnp.sum(probs * grad_probs, -1, keepdims=True)
    grad_scores = (probs * (grad_probs - inner)).astype(jnp.bfloat16)
    grad_query = (jnp.dot(grad_scores, keys, preferred_element_type=jnp.float32) * scale).astype(
        jnp.bfloat16
    )
    grad_keys = (jnp.dot(grad_scores.T, query, preferred_element_type=jnp.float32) * scale).astype(
        jnp.bfloat16
    )
    grad_values = jnp.dot(
        probs.astype(jnp.bfloat16).T, grad_out, preferred_element_type=jnp.float32
    ).astype(jnp.bfloat16)
    return (grad_query, grad_keys, grad_values)


def run_forward(inputs, mask_rows, vectors, attn_mats, mlp_mats):
    ln1_gain, ln1_bias, b_query, b_value, b_out, ln2_gain, ln2_bias, b_fc1, b_fc2 = vectors
    w_query, w_key, w_value, w_out = attn_mats
    w_fc1, w_fc2 = mlp_mats
    clips, local_len, width = inputs.shape
    rows = inputs.reshape(clips * local_len, width).astype(jnp.float32)
    normed1, hat1, inv1 = normalize(rows, ln1_gain, ln1_bias)
    first_in = normed1.astype(jnp.bfloat16)
    head_shape = (clips, local_len, HEADS, HD)
    query = (jnp.dot(first_in, w_query, preferred_element_type=jnp.float32) + b_query).astype(
        jnp.bfloat16
    )
    keys = jnp.dot(first_in, w_key, preferred_element_type=jnp.float32).astype(jnp.bfloat16)
    values = (jnp.dot(first_in, w_value, preferred_element_type=jnp.float32) + b_value).astype(
        jnp.bfloat16
    )
    query_heads, keys_heads, values_heads = (
        lax.all_to_all(query.reshape(head_shape), "seq", split_axis=2, concat_axis=1, tiled=True),
        lax.all_to_all(keys.reshape(head_shape), "seq", split_axis=2, concat_axis=1, tiled=True),
        lax.all_to_all(values.reshape(head_shape), "seq", split_axis=2, concat_axis=1, tiled=True),
    )
    query_pairs = to_pairs(query_heads)
    keys_pairs = to_pairs(keys_heads)
    values_pairs = to_pairs(values_heads)
    mixed_pairs, logsum = lax.map(head_forward, (query_pairs, keys_pairs, values_pairs))
    mixed_tokens = lax.all_to_all(
        from_pairs(mixed_pairs, clips), "seq", split_axis=1, concat_axis=2, tiled=True
    )
    attended = mixed_tokens.reshape(clips * local_len, width)
    branch = jnp.dot(attended, w_out, preferred_element_type=jnp.float32) + b_out
    middle = rows + branch
    normed2, hat2, inv2 = normalize(middle, ln2_gain, ln2_bias)
    second_in = normed2.astype(jnp.bfloat16)
    hidden = jnp.dot(second_in, w_fc1, preferred_element_type=jnp.float32) + b_fc1
    activ = jax.nn.gelu(hidden, approximate=False).astype(jnp.bfloat16)
    final = jnp.dot(activ, w_fc2, preferred_element_type=jnp.float32) + b_fc2
    result = (middle + final) * mask_rows
    saved = (
        first_in,
        hat1,
        inv1,
        query_pairs,
        keys_pairs,
        values_pairs,
        logsum,
        attended,
        second_in,
        hat2,
        inv2,
        hidden,
        activ,
    )
    return (result, saved)


def on_device(
    inputs,
    clip_mask,
    ln1_gain,
    ln1_bias,
    w_query,
    b_query,
    w_key,
    w_value,
    b_value,
    w_out,
    b_out,
    ln2_gain,
    ln2_bias,
    w_fc1,
    b_fc1,
    w_fc2,
    b_fc2,
    cotangent,
):
    clips, local_len, width = inputs.shape
    mask_rows = jnp.repeat(clip_mask.astype(jnp.float32), local_len)[:, None]
    vectors = (ln1_gain, ln1_bias, b_query, b_value, b_out, ln2_gain, ln2_bias, b_fc1, b_fc2)
    attn_mats = (
        lax.all_gather(w_query, "fsdp", axis=0, tiled=True),
        lax.all_gather(w_key, "fsdp", axis=0, tiled=True),
        lax.all_gather(w_value, "fsdp", axis=0, tiled=True),
        lax.all_gather(w_out, "fsdp", axis=0, tiled=True),
    )
    mlp_mats = (
        lax.all_gather(w_fc1, "fsdp", axis=0, tiled=True),
        lax.all_gather(w_fc2, "fsdp", axis=0, tiled=True),
    )
    result, unused = run_forward(inputs, mask_rows, vectors, attn_mats, mlp_mats)
    output = result.reshape(clips, local_len, width).astype(jnp.bfloat16)
    attn_back = (
        lax.all_gather(w_query, "fsdp", axis=0, tiled=True),
        lax.all_gather(w_key, "fsdp", axis=0, tiled=True),
        lax.all_gather(w_value, "fsdp", axis=0, tiled=True),
        lax.all_gather(w_out, "fsdp", axis=0, tiled=True),
    )
    mlp_back = (
        lax.all_gather(w_fc1, "fsdp", axis=0, tiled=True),
        lax.all_gather(w_fc2, "fsdp", axis=0, tiled=True),
    )
    full_query, full_key, full_value, full_out = attn_back
    full_fc1, full_fc2 = mlp_back
    unused_result, saved = run_forward(inputs, mask_rows, vectors, attn_back, mlp_back)
    (
        first_in,
        hat1,
        inv1,
        query_pairs,
        keys_pairs,
        values_pairs,
        logsum,
        attended,
        second_in,
        hat2,
        inv2,
        hidden,
        activ,
    ) = saved
    grad_rows = cotangent.reshape(clips * local_len, width).astype(jnp.float32) * mask_rows
    grad_low = grad_rows.astype(jnp.bfloat16)
    grad_b_fc2 = jnp.sum(grad_rows, 0)
    grad_w_fc2 = jnp.dot(activ.T, grad_low, preferred_element_type=jnp.float32)
    grad_activ = jnp.dot(grad_low, full_fc2.T, preferred_element_type=jnp.float32)
    unused_gelu, gelu_pull = jax.vjp(lambda value: jax.nn.gelu(value, approximate=False), hidden)
    grad_hidden = gelu_pull(grad_activ)[0].astype(jnp.bfloat16)
    grad_w_fc1 = jnp.dot(second_in.T, grad_hidden, preferred_element_type=jnp.float32)
    grad_b_fc1 = jnp.sum(grad_hidden.astype(jnp.float32), 0)
    grad_second = jnp.dot(grad_hidden, full_fc1.T, preferred_element_type=jnp.float32)
    grad_ln2_gain = jnp.sum(grad_second * hat2, 0)
    grad_ln2_bias = jnp.sum(grad_second, 0)
    grad_middle = grad_rows + norm_grad(grad_second, hat2, inv2, ln2_gain)
    grad_branch = grad_middle.astype(jnp.bfloat16)
    grad_w_out = jnp.dot(attended.T, grad_branch, preferred_element_type=jnp.float32)
    grad_b_out = jnp.sum(grad_branch.astype(jnp.float32), 0)
    grad_mixed = jnp.dot(grad_branch, full_out.T, preferred_element_type=jnp.float32).astype(
        jnp.bfloat16
    )
    grad_mixed_heads = lax.all_to_all(
        grad_mixed.reshape(clips, local_len, HEADS, HD),
        "seq",
        split_axis=2,
        concat_axis=1,
        tiled=True,
    )
    grad_q_pairs, grad_k_pairs, grad_v_pairs = lax.map(
        head_backward, (query_pairs, keys_pairs, values_pairs, to_pairs(grad_mixed_heads), logsum)
    )
    grad_query, grad_keys, grad_values = (
        lax.all_to_all(
            from_pairs(grad_q_pairs, clips), "seq", split_axis=1, concat_axis=2, tiled=True
        ),
        lax.all_to_all(
            from_pairs(grad_k_pairs, clips), "seq", split_axis=1, concat_axis=2, tiled=True
        ),
        lax.all_to_all(
            from_pairs(grad_v_pairs, clips), "seq", split_axis=1, concat_axis=2, tiled=True
        ),
    )
    grad_query = grad_query.reshape(clips * local_len, width)
    grad_keys = grad_keys.reshape(clips * local_len, width)
    grad_values = grad_values.reshape(clips * local_len, width)
    grad_w_query = jnp.dot(first_in.T, grad_query, preferred_element_type=jnp.float32)
    grad_w_key = jnp.dot(first_in.T, grad_keys, preferred_element_type=jnp.float32)
    grad_w_value = jnp.dot(first_in.T, grad_values, preferred_element_type=jnp.float32)
    grad_b_query = jnp.sum(grad_query.astype(jnp.float32), 0)
    grad_b_value = jnp.sum(grad_values.astype(jnp.float32), 0)
    grad_first = (
        jnp.dot(grad_query, full_query.T, preferred_element_type=jnp.float32)
        + jnp.dot(grad_keys, full_key.T, preferred_element_type=jnp.float32)
        + jnp.dot(grad_values, full_value.T, preferred_element_type=jnp.float32)
    )
    grad_ln1_gain = jnp.sum(grad_first * hat1, 0)
    grad_ln1_bias = jnp.sum(grad_first, 0)
    grad_inputs = grad_middle + norm_grad(grad_first, hat1, inv1, ln1_gain)
    grad_inputs = grad_inputs.reshape(clips, local_len, width)
    all_grads = (
        grad_ln1_gain,
        grad_ln1_bias,
        grad_w_query,
        grad_b_query,
        grad_w_key,
        grad_w_value,
        grad_b_value,
        grad_w_out,
        grad_b_out,
        grad_ln2_gain,
        grad_ln2_bias,
        grad_w_fc1,
        grad_b_fc1,
        grad_w_fc2,
        grad_b_fc2,
    )
    owned = (
        lax.psum_scatter(all_grads[0], ("fsdp", "seq"), scatter_dimension=0, tiled=True),
        lax.psum_scatter(all_grads[1], ("fsdp", "seq"), scatter_dimension=0, tiled=True),
        lax.psum_scatter(all_grads[2], ("fsdp", "seq"), scatter_dimension=0, tiled=True),
        lax.psum_scatter(all_grads[3], ("fsdp", "seq"), scatter_dimension=0, tiled=True),
        lax.psum_scatter(all_grads[4], ("fsdp", "seq"), scatter_dimension=0, tiled=True),
        lax.psum_scatter(all_grads[5], ("fsdp", "seq"), scatter_dimension=0, tiled=True),
        lax.psum_scatter(all_grads[6], ("fsdp", "seq"), scatter_dimension=0, tiled=True),
        lax.psum_scatter(all_grads[7], ("fsdp", "seq"), scatter_dimension=0, tiled=True),
        lax.psum_scatter(all_grads[8], ("fsdp", "seq"), scatter_dimension=0, tiled=True),
        lax.psum_scatter(all_grads[9], ("fsdp", "seq"), scatter_dimension=0, tiled=True),
        lax.psum_scatter(all_grads[10], ("fsdp", "seq"), scatter_dimension=0, tiled=True),
        lax.psum_scatter(all_grads[11], ("fsdp", "seq"), scatter_dimension=0, tiled=True),
        lax.psum_scatter(all_grads[12], ("fsdp", "seq"), scatter_dimension=0, tiled=True),
        lax.psum_scatter(all_grads[13], ("fsdp", "seq"), scatter_dimension=0, tiled=True),
        lax.psum_scatter(all_grads[14], ("fsdp", "seq"), scatter_dimension=0, tiled=True),
    )
    return (
        output,
        grad_inputs,
        owned[0],
        owned[1],
        owned[2],
        owned[3],
        owned[4],
        owned[5],
        owned[6],
        owned[7],
        owned[8],
        owned[9],
        owned[10],
        owned[11],
        owned[12],
        owned[13],
        owned[14],
    )


def solution(mesh):
    return jax.shard_map(
        on_device,
        mesh=mesh,
        in_specs=(
            P("fsdp", "seq", None),
            P("fsdp"),
            P(),
            P(),
            P("fsdp", None),
            P(),
            P("fsdp", None),
            P("fsdp", None),
            P(),
            P("fsdp", None),
            P(),
            P(),
            P(),
            P("fsdp", None),
            P(),
            P("fsdp", None),
            P(),
            P("fsdp", "seq", None),
        ),
        out_specs=(
            P("fsdp", "seq", None),
            P("fsdp", "seq", None),
            P(("fsdp", "seq")),
            P(("fsdp", "seq")),
            P(("fsdp", "seq"), None),
            P(("fsdp", "seq")),
            P(("fsdp", "seq"), None),
            P(("fsdp", "seq"), None),
            P(("fsdp", "seq")),
            P(("fsdp", "seq"), None),
            P(("fsdp", "seq")),
            P(("fsdp", "seq")),
            P(("fsdp", "seq")),
            P(("fsdp", "seq"), None),
            P(("fsdp", "seq")),
            P(("fsdp", "seq"), None),
            P(("fsdp", "seq")),
        ),
        check_vma=False,
    )
```

profile of v0, /device:TPU:0, one launch (start us, length us, event | category | flops | bytes accessed | tf_op | source)
XLA Modules:
  0.0 1689.8 jit_solution(14784483086480142402)
XLA Ops:
  13.5 27.1 %all-gather.7.cloned.1.call-done = bf16[1024,1024]{1,0:T(8,128)(2,1)} async-done(((bf16[128,1024]{1,0:T(8,128)(2,1)}), bf16[1024,1024]{1,0:T(8,128)(2,1)}) %all-gather.7.cloned.1.call-update) | async-done | bytes 2097168 | tf_op jit(solution)/shard_map/all_gather | solution.py:149
  49.5 20.9 %all-gather.9.cloned.1.call-done = bf16[1024,1024]{1,0:T(8,128)(2,1)} async-done(((bf16[128,1024]{1,0:T(8,128)(2,1)}), bf16[1024,1024]{1,0:T(8,128)(2,1)}) %all-gather.9.cloned.1.call-update) | async-done | bytes 2097168 | tf_op jit(solution)/shard_map/all_gather | solution.py:150
  79.9 20.3 %all-gather.11.cloned.1.call-done = bf16[1024,1024]{1,0:T(8,128)(2,1)} async-done(((bf16[128,1024]{1,0:T(8,128)(2,1)}), bf16[1024,1024]{1,0:T(8,128)(2,1)}) %all-gather.11.cloned.1.call-update) | async-done | bytes 2097168 | tf_op jit(solution)/shard_map/all_gather | solution.py:151
  113.1 22.1 %all-to-all-done.2 = bf16[1,392,16,64]{1,3,0,2:T(8,128)(2,1)} async-done(((bf16[1,392,16,64]{1,3,0,2:T(8,128)(2,1)}), bf16[1,392,16,64]{1,3,0,2:T(8,128)(2,1)}, u32[]{:S(2)}, u32[]{:S(2)}) %all-to-all-start.2) | async-done | bytes 802848 | tf_op jit(solution)/shard_map/all_to_all | solution.py:89
  138.7 29.4 %while.37 = (s32[]{:T(128)}, bf16[4,1568,64]{1,2,0:T(8,128)(2,1)}, f32[4,1568]{1,0:T(4,128)S(1)}, bf16[4,1568,64]{2,1,0:T(8,128)(2,1)S(1)}, bf16[4,1568,64]{2,1,...) while((s32[]{:T(128)}, bf16[4,1568,64]{1,2,0:T(8,128)(2,1)}, ...), condition=%wide.region_11.12_spmd, body=%wide.region_8.0_spmd.sunk | while | flops 651634176 | bytes 30998112 | solution.py:94
  183.5 19.4 %all-to-all-done.4 = bf16[4,2,50176]{2,1,0:T(2,128)(2,1)} async-done(((bf16[4,2,50176]{2,1,0:T(2,128)(2,1)}), bf16[4,2,50176]{2,1,0:T(2,128)(2,1)}, u32[]{:S(2)}, u32[]{:S(2)}) %all-to-all-start.4) | async-done | bytes 802848 | tf_op jit(solution)/shard_map/all_to_all | solution.py:95
  215.6 21.5 %fusion.70 = (f32[392,4096]{1,0:T(8,128)}, f32[392,4096]{1,0:T(8,128)}) fusion(f32[4096]{0:T(1024)S(1)} %copy-done.16, bf16[1024,4096]{1,0:T(8,128)(2,1)} %all-gather.15.cloned.1.call-done, f32[392,1024]{1,0:T(8,128)} %copy-done.4, f32[392]{0:T(512)S(1)} %add_rsqrt_fusion, f32[392]{0:T(512)S(1)} %broadcast_multiply_fusion.4, f32[1024]{0:T(1024)S(1)} %copy-done.45, ...), kind=kOutput, calls=%fused_computation.79 | convolution fusion | flops 3391496192 | bytes 22867008 | tf_op jit(solution)/shard_map/dot_general | solution.py:103
  242.2 11.8 convert_reduce_fusion
  274.7 34.4 %all-to-all-done.5 = bf16[1,392,16,64]{1,3,0,2:T(8,128)(2,1)} async-done(((bf16[1,392,16,64]{1,3,0,2:T(8,128)(2,1)}), bf16[1,392,16,64]{1,3,0,2:T(8,128)(2,1)}, u32[]{:S(2)}, u32[]{:S(2)}) %all-to-all-start.5) | async-done | bytes 802848 | tf_op jit(solution)/shard_map/all_to_all | solution.py:207
  315.2 131.6 %while.38 = (s32[]{:T(128)}, bf16[4,1568,64]{1,2,0:T(8,128)(2,1)}, bf16[4,1568,64]{1,2,0:T(8,128)(2,1)}, bf16[4,1568,64]{1,2,0:T(8,128)(2,1)}, bf16[4,1568,64]{2...) while((s32[]{:T(128)}, bf16[4,1568,64]{1,2,0:T(8,128)(2,1)}, ...), condition=%wide.region_18.19_spmd, body=%wide.region_16.18_spmd.sunk | while | flops 1593688576 | bytes 157126304 | solution.py:214
  324.8 10.5 multiply_convert_fusion.5
  423.6 10.5 multiply_convert_fusion.5
  457.1 21.4 %all_to_all.162 = bf16[4,2,50176]{2,1,0:T(2,128)(2,1)} all-to-all(bf16[4,2,50176]{2,1,0:T(2,128)(2,1)} %reshape.302), channel_id=1, replica_groups=mesh['fsdp'=8,'seq'=4] {'seq'}, dimensions={0} | all-to-all | bytes 1605632 | tf_op jit(solution)/shard_map/all_to_all | solution.py:218
  501.9 40.5 %all_to_all.163 = bf16[4,2,50176]{2,1,0:T(2,128)(2,1)} all-to-all(bf16[4,2,50176]{2,1,0:T(2,128)(2,1)} %reshape.304), channel_id=1, replica_groups=mesh['fsdp'=8,'seq'=4] {'seq'}, dimensions={0} | all-to-all | bytes 1605632 | tf_op jit(solution)/shard_map/all_to_all | solution.py:221
  565.8 39.4 %all_to_all.164 = bf16[4,2,50176]{2,1,0:T(2,128)(2,1)} all-to-all(bf16[4,2,50176]{2,1,0:T(2,128)(2,1)} %reshape.306), channel_id=1, replica_groups=mesh['fsdp'=8,'seq'=4] {'seq'}, dimensions={0} | all-to-all | bytes 1605632 | tf_op jit(solution)/shard_map/all_to_all | solution.py:224
  619.0 13.0 fusion.182
  632.7 15.5 fusion.83
  649.1 28.9 %while.36 = (s32[]{:T(128)}, bf16[4,1568,64]{1,2,0:T(8,128)(2,1)}, bf16[4,1568,64]{2,1,0:T(8,128)(2,1)S(1)}, bf16[4,1568,64]{2,1,0:T(8,128)(2,1)S(1)}, bf16[4,1568,64]{2,1,0:T(8,128)(2,1)}, /*index=5*/s32[]{:T(128)}) while((s32[]{:T(128)}, bf16[4,1568,64]{1,2,0:T(8,128)(2,1)}, bf16[4,1568,64]{2,1,0:T(8,128)(2,1)S(1)}, ...), condition=%wide.region_5.6_spmd, body=%wide.region_2.5_spmd.sunk | while | flops 651632576 | bytes 30954188 | solution.py:94
  690.8 33.4 %all-to-all-done.3 = bf16[4,2,50176]{2,1,0:T(2,128)(2,1)S(1)} async-done(((bf16[4,2,50176]{2,1,0:T(2,128)(2,1)}), bf16[4,2,50176]{2,1,0:T(2,128)(2,1)S(1)}, u32[]{:S(2)}, u32[]{:S(2)}) %all-to-all-start.3) | async-done | bytes 802848 | tf_op jit(solution)/shard_map/all_to_all | solution.py:95
  730.1 26.3 %fusion.137 = bf16[1,392,1024]{2,1,0:T(8,128)(2,1)} fusion(f32[392,1024]{1,0:T(8,128)S(1)} %get-tuple-element.198, bf16[4096,1024]{1,0:T(8,128)(2,1)} %all-gather.17.cloned.1.call-done, bf16[1024,4096]{1,0:T(8,128)(2,1)} %all-gather.15.cloned.1.call-done, f32[4096]{0:T(1024)S(1)} %copy-done.17, f32[]{:T(128)} %bitcast.42, f32[1024]{0:T(1024)S(1)} %copy-done.44, ...), kind=kOutput, calls=%fused_computation.189 | convolution fusion | flops 6686253056 | bytes 19217476 | tf_op jit(solution)/shard_map/dot_general | solution.py:105
  766.5 39.0 %all-reduce.9 = (f32[1024]{0:T(1024)S(1)}, f32[1024]{0:T(1024)S(1)}, f32[1024]{0:T(1024)S(1)}, f32[1024]{0:T(1024)S(1)}, f32[1024]{0:T(1024)S(1)}, /*index=5*/f3...) all-reduce(f32[1024]{0:T(1024)S(1)} %get-tuple-element.134, ...), channel_id=2, replica_groups=mesh['fsdp'=8,'seq'=4] {'fsdp','seq'}, use_global_device_ids=true, to_apply=%region_22.23.clone | all-reduce | flops 12288 | bytes 98304
  813.9 138.1 %reduce-scatter.11.cloned.1.call-done = f32[32,1024]{1,0:T(8,128)} async-done(((f32[1024,1024]{1,0:T(8,128)}), f32[32,1024]{1,0:T(8,128)}) %reduce-scatter.11.cloned.1.call-update) | async-done | bytes 131088 | tf_op jit(solution)/shard_map/reduce_scatter | solution.py:268
  952.1 365.8 %reduce-scatter.15.cloned.1.call-done = f32[32,4096]{1,0:T(8,128)} async-done(((f32[1024,4096]{1,0:T(8,128)}), f32[32,4096]{1,0:T(8,128)}) %reduce-scatter.15.cloned.1.call-update) | async-done | bytes 524304 | tf_op jit(solution)/shard_map/reduce_scatter | solution.py:274
  1317.9 364.9 %reduce-scatter.17.cloned.1.call-done = f32[128,1024]{1,0:T(8,128)} async-done(((f32[4096,1024]{1,0:T(8,128)}), f32[128,1024]{1,0:T(8,128)}) %reduce-scatter.17.cloned.1.call-update) | async-done | bytes 524304 | tf_op jit(solution)/shard_map/reduce_scatter | solution.py:276
  (292 shorter events, 378.2 us)
Async XLA Ops:
  7.2 33.4 %all-gather.7.cloned.1.call-start = ((), (), s32[]{:S(2)}) async-start(), calls=%async_computation.15 | async-start | bytes 2359296 | tf_op jit(solution)/shard_map/all_gather | solution.py:149
  7.9 62.4 %all-gather.9.cloned.1.call-start = ((), (), s32[]{:S(2)}) async-start(), calls=%async_computation.16 | async-start | bytes 2359296 | tf_op jit(solution)/shard_map/all_gather | solution.py:150
  8.7 91.5 %all-gather.11.cloned.1.call-start = ((), (), s32[]{:S(2)}) async-start(), calls=%async_computation.17 | async-start | bytes 2359296 | tf_op jit(solution)/shard_map/all_gather | solution.py:151
  9.4 201.4 %all-gather.13.cloned.1.call-start = ((), (), s32[]{:S(2)}) async-start(), calls=%async_computation.18 | async-start | bytes 2359296 | tf_op jit(solution)/shard_map/all_gather | solution.py:152
  10.0 205.6 %all-gather.15.cloned.1.call-start = ((), (), s32[]{:S(2)}) async-start(), calls=%async_computation.19 | async-start | bytes 9437184 | tf_op jit(solution)/shard_map/all_gather | solution.py:155
  11.9 88.3 %copy-start.18 = (f32[392]{0:T(512)}, f32[392]{0:T(512)S(1)}, u32[]{:S(2)}) copy-start(f32[392]{0:T(512)S(1)} %broadcast_multiply_fusion.6) | copy-start | bytes 4708
  13.4 86.8 %copy-start.25 = (f32[392]{0:T(512)}, f32[392]{0:T(512)S(1)}, u32[]{:S(2)}) copy-start(f32[392]{0:T(512)S(1)} %add_rsqrt_fusion.2) | copy-start | bytes 4708
  13.4 56.9 %copy-start.2 = (bf16[1,392,1024]{2,1,0:T(8,128)(2,1)S(1)}, bf16[1,392,1024]{2,1,0:T(8,128)(2,1)}, u32[]{:S(2)}) copy-start(bf16[1,392,1024]{2,1,0:T(8,128)(2,1)} %param.24) | copy-start | bytes 2408452
  13.4 56.9 %copy-start.30 = (f32[1024]{0:T(1024)S(1)}, f32[1024]{0:T(1024)}, u32[]{:S(2)}) copy-start(f32[1024]{0:T(1024)} %param.26) | copy-start | bytes 12292
  13.4 56.9 %copy-start.42 = (f32[1024]{0:T(1024)S(1)}, f32[1024]{0:T(1024)}, u32[]{:S(2)}) copy-start(f32[1024]{0:T(1024)} %param.27) | copy-start | bytes 12292
  44.8 30.8 %all-to-all-start = ((bf16[1,392,16,64]{1,3,0,2:T(8,128)(2,1)}), bf16[1,392,16,64]{1,3,0,2:T(8,128)(2,1)S(1)}, u32[]{:S(2)}, u32[]{:S(2)}) async-start(bf16[1,392,16,64]{1,3,0,2:T(8,128)(2,1)} %bitcast.17), calls=%async_computation | async-start | bytes 2097152 | tf_op jit(solution)/shard_map/all_to_all | solution.py:87
  49.5 50.7 %copy-start.41 = (f32[1024]{0:T(1024)S(1)}, f32[1024]{0:T(1024)}, u32[]{:S(2)}) copy-start(f32[1024]{0:T(1024)} %param.32) | copy-start | bytes 12292
  75.6 29.7 %all-to-all-start.1 = ((bf16[1,392,16,64]{1,3,0,2:T(8,128)(2,1)}), bf16[1,392,16,64]{1,3,0,2:T(8,128)(2,1)}, u32[]{:S(2)}, u32[]{:S(2)}) async-start(bf16[1,392,16,64]{1,3,0,2:T(8,128)(2,1)} %bitcast.24), calls=%async_computation.1 | async-start | bytes 2097152 | tf_op jit(solution)/shard_map/all_to_all | solution.py:88
  105.3 29.8 %all-to-all-start.2 = ((bf16[1,392,16,64]{1,3,0,2:T(8,128)(2,1)}), bf16[1,392,16,64]{1,3,0,2:T(8,128)(2,1)}, u32[]{:S(2)}, u32[]{:S(2)}) async-start(bf16[1,392,16,64]{1,3,0,2:T(8,128)(2,1)} %bitcast.31), calls=%async_computation.2 | async-start | bytes 2097152 | tf_op jit(solution)/shard_map/all_to_all | solution.py:89
  109.6 132.6 %all-gather.17.cloned.1.call-start = ((), (), s32[]{:S(2)}) async-start(), calls=%async_computation.20 | async-start | bytes 9437184 | tf_op jit(solution)/shard_map/all_gather | solution.py:156
  178.4 24.5 %all-to-all-start.4 = ((bf16[4,2,50176]{2,1,0:T(2,128)(2,1)}), bf16[4,2,50176]{2,1,0:T(2,128)(2,1)}, u32[]{:S(2)}, u32[]{:S(2)}) async-start(bf16[4,2,50176]{2,1,0:T(2,128)(2,1)} %reshape.300), calls=%async_computation.4 | async-start | bytes 1605632 | tf_op jit(solution)/shard_map/all_to_all | solution.py:95
  265.1 44.0 %all-to-all-start.5 = ((bf16[1,392,16,64]{1,3,0,2:T(8,128)(2,1)}), bf16[1,392,16,64]{1,3,0,2:T(8,128)(2,1)}, u32[]{:S(2)}, u32[]{:S(2)}) async-start(bf16[1,392,16,64]{1,3,0,2:T(8,128)(2,1)} %bitcast.308), calls=%async_computation.5 | async-start | bytes 2097152 | tf_op jit(solution)/shard_map/all_to_all | solution.py:207
  269.7 544.2 %reduce-scatter.13.cloned.1.call-start = ((), (), s32[]{:S(2)}) async-start(), calls=%async_computation.24 | async-start | bytes 4325376 | tf_op jit(solution)/shard_map/reduce_scatter | solution.py:270
  274.7 539.2 %reduce-scatter.7.cloned.1.call-start = ((), (), s32[]{:S(2)}) async-start(), calls=%async_computation.21 | async-start | bytes 4325376 | tf_op jit(solution)/shard_map/reduce_scatter | solution.py:265
  491.5 322.4 %reduce-scatter.9.cloned.1.call-start = ((), (), s32[]{:S(2)}) async-start(), calls=%async_computation.22 | async-start | bytes 4325376 | tf_op jit(solution)/shard_map/reduce_scatter | solution.py:267
  555.5 396.6 %reduce-scatter.11.cloned.1.call-start = ((), (), s32[]{:S(2)}) async-start(), calls=%async_computation.23 | async-start | bytes 4325376 | tf_op jit(solution)/shard_map/reduce_scatter | solution.py:268
  618.3 699.6 %reduce-scatter.15.cloned.1.call-start = ((), (), s32[]{:S(2)}) async-start(), calls=%async_computation.25 | async-start | bytes 17301504 | tf_op jit(solution)/shard_map/reduce_scatter | solution.py:274
  632.0 1050.8 %reduce-scatter.17.cloned.1.call-start = ((), (), s32[]{:S(2)}) async-start(), calls=%async_computation.26 | async-start | bytes 17301504 | tf_op jit(solution)/shard_map/reduce_scatter | solution.py:276
  686.8 37.4 %all-to-all-start.3 = ((bf16[4,2,50176]{2,1,0:T(2,128)(2,1)}), bf16[4,2,50176]{2,1,0:T(2,128)(2,1)S(1)}, u32[]{:S(2)}, u32[]{:S(2)}) async-start(bf16[4,2,50176]{2,1,0:T(2,128)(2,1)} %reshape.298), calls=%async_computation.3 | async-start | bytes 1605632 | tf_op jit(solution)/shard_map/all_to_all | solution.py:95
  (49 other events, 578.2 us)
Sparse Core Ops, SparseCore 0:
  9.9 30.5 all-gather.6
  42.4 27.8 all-gather.8
  72.2 27.8 all-gather.10
  101.9 27.8 all-gather.12
  131.6 54.4 all-gather.14
  187.8 54.3 all-gather.16
  274.8 153.5 reduce-scatter.12
  491.7 155.6 reduce-scatter.6
  650.2 152.9 reduce-scatter.8
  805.8 146.1 reduce-scatter.10
  954.9 362.8 reduce-scatter.14
  1320.6 362.1 reduce-scatter.16
where the time goes:
time: 1700 us; the launch traced here: 1690 us
  waiting for transfers between devices  1060 us (62%)
  matrix products  265 us (16%)
  blocking collectives  140 us (8%)
  local copies, waits for them, and re-layouts  119 us (7%)
  other arithmetic  65.8 us (4%)
  starting transfers between devices  26.8 us (2%)
    reduce_scatter x1, waiting for transfers between devices, on_device(): lax.psum_scatter(all_grads[11], ('fsdp', 'seq'), scatter_dimension=0, til...  366 us
    reduce_scatter x1, waiting for transfers between devices, on_device(): lax.psum_scatter(all_grads[13], ('fsdp', 'seq'), scatter_dimension=0, til...  365 us
    reduce_scatter x1, waiting for transfers between devices, on_device(): lax.psum_scatter(all_grads[5], ('fsdp', 'seq'), scatter_dimension=0, tile...  138 us
    unnamed x118, local copies, waits for them, and re-layouts  58 us
    all_to_all x2, waiting for transfers between devices, run_forward(): lax.all_to_all(from_pairs(mixed_pairs, clips), 'seq', split_axis=1, conca...  52.8 us
    convert_element_type x4, other arithmetic, head_backward(): grad_scores = (probs * (grad_probs - inner)).astype(jnp.bfloat16)  41.9 us
    all_to_all x1, blocking collectives, on_device(): lax.all_to_all(from_pairs(grad_k_pairs, clips), 'seq', split_axis=1, conc...  40.5 us
    all_to_all x1, blocking collectives, on_device(): lax.all_to_all(from_pairs(grad_v_pairs, clips), 'seq', split_axis=1, conc...  39.4 us
  transfers between devices with their start and end apart: 18, of which 13 were waited for; matrix products, arithmetic and copies ran while one was open for 25% of the time, Pallas kernels for 0%

commit v1 on v0

--- a/solution.py
+++ b/solution.py
@@ -6,6 +6,29 @@
 HEADS = 16
 HD = 64
 EPSILON = 1e-06
+
+
+def cut_along(value, dim, size):
+    shape = value.shape
+    blocks = value.reshape(*shape[:dim], size, shape[dim] // size, *shape[dim + 1 :])
+    return jnp.moveaxis(blocks, dim, 0)
+
+
+def in_order(tiles, dim):
+    tiles = jnp.moveaxis(tiles, 0, dim)
+    shape = tiles.shape
+    return tiles.reshape(*shape[:dim], shape[dim] * shape[dim + 1], *shape[dim + 2 :])
+
+
+def exchange_directly(value, axis, split_dim, concat_dim):
+    peers, here = (lax.axis_size(axis), lax.axis_index(axis))
+    blocks = cut_along(value, split_dim, peers)
+    finished = [blocks[here]]
+    for lap in range(1, peers):
+        sent = blocks[(here + lap) % peers]
+        finished.append(lax.ppermute(sent, axis, [(i, (i + lap) % peers) for i in range(peers)]))
+    blocks = jnp.stack(finished)[(here - jnp.arange(peers)) % peers]
+    return in_order(blocks, concat_dim)
 
 
 def normalize(rows, gain, shift):
@@ -204,12 +227,8 @@
     grad_mixed = jnp.dot(grad_branch, full_out.T, preferred_element_type=jnp.float32).astype(
         jnp.bfloat16
     )
-    grad_mixed_heads = lax.all_to_all(
-        grad_mixed.reshape(clips, local_len, HEADS, HD),
-        "seq",
-        split_axis=2,
-        concat_axis=1,
-        tiled=True,
+    grad_mixed_heads = exchange_directly(
+        grad_mixed.reshape(clips, local_len, HEADS, HD), "seq", 2, 1
     )
     grad_q_pairs, grad_k_pairs, grad_v_pairs = lax.map(
         head_backward, (query_pairs, keys_pairs, values_pairs, to_pairs(grad_mixed_heads), logsum)

time: 1700 us -> 1700 us (level)
    all_to_all x1 -> x0, waiting for transfers between devices: 34.4 us -> none  [on_device(): lax.all_to_all(grad_mixed.reshape(clips, local_len, HEADS, HD), 'seq', sp...]
    ppermute x0 -> x3, waiting for transfers between devices: none -> 25.6 us  [exchange_directly(): lax.ppermute(sent, axis, [(i, (i + lap) % peers) for i in range(peers)])]
    unnamed x118 -> x116, local copies, waits for them, and re-layouts: 58 us -> 58 us
  transfers between devices with their start and end apart: 18 -> 20, of which waited for: 13 -> 14; matrix products, arithmetic and copies ran while one was open for 25% -> 25% of each run, Pallas kernels for 0% -> 0%
where the time goes in v1:
time: 1700 us
  waiting for transfers between devices  1050 us (62%)
  matrix products  265 us (16%)
  blocking collectives  146 us (9%)
  local copies, waits for them, and re-layouts  129 us (8%)
  other arithmetic  69.3 us (4%)
  starting transfers between devices  26.4 us (2%)
    reduce_scatter x1, waiting for transfers between devices, on_device(): lax.psum_scatter(all_grads[11], ('fsdp', 'seq'), scatter_dimension=0, til...  366 us
    reduce_scatter x1, waiting for transfers between devices, on_device(): lax.psum_scatter(all_grads[13], ('fsdp', 'seq'), scatter_dimension=0, til...  365 us
    reduce_scatter x1, waiting for transfers between devices, on_device(): lax.psum_scatter(all_grads[5], ('fsdp', 'seq'), scatter_dimension=0, tile...  135 us
    unnamed x116, local copies, waits for them, and re-layouts  58 us
    all_to_all x2, waiting for transfers between devices, run_forward(): lax.all_to_all(from_pairs(mixed_pairs, clips), 'seq', split_axis=1, conca...  53.2 us
    convert_element_type x4, other arithmetic, head_backward(): grad_scores = (probs * (grad_probs - inner)).astype(jnp.bfloat16)  41.9 us
    all_to_all x1, blocking collectives, on_device(): lax.all_to_all(from_pairs(grad_k_pairs, clips), 'seq', split_axis=1, conc...  41.5 us
    all_to_all x1, blocking collectives, on_device(): lax.all_to_all(from_pairs(grad_v_pairs, clips), 'seq', split_axis=1, conc...  40.3 us
  transfers between devices with their start and end apart: 20, of which 14 were waited for; matrix products, arithmetic and copies ran while one was open for 25% of the time, Pallas kernels for 0%

profile of v1, /device:TPU:0, one launch (start us, length us, event | category | flops | bytes accessed | tf_op | source)
XLA Modules:
  0.0 1696.5 jit_solution(529424338691992760)
XLA Ops:
  13.5 27.1 %all-gather.7.cloned.1.call-done = bf16[1024,1024]{1,0:T(8,128)(2,1)} async-done(((bf16[128,1024]{1,0:T(8,128)(2,1)}), bf16[1024,1024]{1,0:T(8,128)(2,1)}) %all-gather.7.cloned.1.call-update) | async-done | bytes 2097168 | tf_op jit(solution)/shard_map/all_gather | solution.py:172
  49.5 20.9 %all-gather.9.cloned.1.call-done = bf16[1024,1024]{1,0:T(8,128)(2,1)} async-done(((bf16[128,1024]{1,0:T(8,128)(2,1)}), bf16[1024,1024]{1,0:T(8,128)(2,1)}) %all-gather.9.cloned.1.call-update) | async-done | bytes 2097168 | tf_op jit(solution)/shard_map/all_gather | solution.py:173
  79.8 20.3 %all-gather.11.cloned.1.call-done = bf16[1024,1024]{1,0:T(8,128)(2,1)} async-done(((bf16[128,1024]{1,0:T(8,128)(2,1)}), bf16[1024,1024]{1,0:T(8,128)(2,1)}) %all-gather.11.cloned.1.call-update) | async-done | bytes 2097168 | tf_op jit(solution)/shard_map/all_gather | solution.py:174
  113.1 22.1 %all-to-all-done.2 = bf16[1,392,16,64]{1,3,0,2:T(8,128)(2,1)} async-done(((bf16[1,392,16,64]{1,3,0,2:T(8,128)(2,1)}), bf16[1,392,16,64]{1,3,0,2:T(8,128)(2,1)}, u32[]{:S(2)}, u32[]{:S(2)}) %all-to-all-start.2) | async-done | bytes 802848 | tf_op jit(solution)/shard_map/all_to_all | solution.py:112
  138.7 29.5 %while.37 = (s32[]{:T(128)}, bf16[4,1568,64]{1,2,0:T(8,128)(2,1)}, f32[4,1568]{1,0:T(4,128)S(1)}, bf16[4,1568,64]{2,1,0:T(8,128)(2,1)S(1)}, bf16[4,1568,64]{2,1,...) while((s32[]{:T(128)}, bf16[4,1568,64]{1,2,0:T(8,128)(2,1)}, ...), condition=%wide.region_11.12_spmd, body=%wide.region_8.0_spmd.sunk | while | flops 651634176 | bytes 30998112 | solution.py:117
  183.7 19.1 %all-to-all-done.4 = bf16[4,2,50176]{2,1,0:T(2,128)(2,1)} async-done(((bf16[4,2,50176]{2,1,0:T(2,128)(2,1)}), bf16[4,2,50176]{2,1,0:T(2,128)(2,1)}, u32[]{:S(2)}, u32[]{:S(2)}) %all-to-all-start.4) | async-done | bytes 802848 | tf_op jit(solution)/shard_map/all_to_all | solution.py:118
  215.5 21.5 %fusion.70 = (f32[392,4096]{1,0:T(8,128)}, f32[392,4096]{1,0:T(8,128)}) fusion(f32[4096]{0:T(1024)S(1)} %copy-done.15, bf16[1024,4096]{1,0:T(8,128)(2,1)} %all-gather.15.cloned.1.call-done, f32[392,1024]{1,0:T(8,128)} %copy-done.4, f32[392]{0:T(512)S(1)} %add_rsqrt_fusion, f32[392]{0:T(512)S(1)} %broadcast_multiply_fusion.4, f32[1024]{0:T(1024)S(1)} %copy-done.44, ...), kind=kOutput, calls=%fused_computation.80 | convolution fusion | flops 3391496192 | bytes 22867008 | tf_op jit(solution)/shard_map/dot_general | solution.py:126
  242.2 11.8 convert_reduce_fusion
  277.6 24.6 %collective-permute-done.1 = bf16[1,392,4,64]{1,3,2,0:T(8,128)(2,1)} collective-permute-done((bf16[1,392,4,64]{1,3,2,0:T(8,128)(2,1)}, bf16[1,392,4,64]{1,3,2,0:T(8,128)(2,1)}, u32[]{:S(2)}, u32[]{:S(2)}) %collective-permute-start.1) | collective-permute-done | bytes 200736 | tf_op jit(solution)/shard_map/ppermute | solution.py:29
  316.9 131.2 %while.38 = (s32[]{:T(128)}, bf16[4,1568,64]{1,2,0:T(8,128)(2,1)}, bf16[4,1568,64]{1,2,0:T(8,128)(2,1)}, bf16[4,1568,64]{1,2,0:T(8,128)(2,1)}, bf16[4,1568,64]{2...) while((s32[]{:T(128)}, bf16[4,1568,64]{1,2,0:T(8,128)(2,1)}, ...), condition=%wide.region_18.19_spmd, body=%wide.region_16.18_spmd.sunk | while | flops 1593688576 | bytes 156749472 | solution.py:233
  392.1 10.5 multiply_convert_fusion.5
  424.9 10.5 multiply_convert_fusion.5
  458.4 25.4 %all_to_all.144 = bf16[4,2,50176]{2,1,0:T(2,128)(2,1)} all-to-all(bf16[4,2,50176]{2,1,0:T(2,128)(2,1)} %reshape.365), channel_id=1, replica_groups=mesh['fsdp'=8,'seq'=4] {'seq'}, dimensions={0} | all-to-all | bytes 1605632 | tf_op jit(solution)/shard_map/all_to_all | solution.py:237
  507.4 41.5 %all_to_all.145 = bf16[4,2,50176]{2,1,0:T(2,128)(2,1)} all-to-all(bf16[4,2,50176]{2,1,0:T(2,128)(2,1)} %reshape.367), channel_id=1, replica_groups=mesh['fsdp'=8,'seq'=4] {'seq'}, dimensions={0} | all-to-all | bytes 1605632 | tf_op jit(solution)/shard_map/all_to_all | solution.py:240
  572.3 40.3 %all_to_all.146 = bf16[4,2,50176]{2,1,0:T(2,128)(2,1)} all-to-all(bf16[4,2,50176]{2,1,0:T(2,128)(2,1)} %reshape.369), channel_id=1, replica_groups=mesh['fsdp'=8,'seq'=4] {'seq'}, dimensions={0} | all-to-all | bytes 1605632 | tf_op jit(solution)/shard_map/all_to_all | solution.py:243
  626.4 13.0 fusion.184
  640.1 15.5 fusion.83
  656.6 28.9 %while.36 = (s32[]{:T(128)}, bf16[4,1568,64]{1,2,0:T(8,128)(2,1)}, bf16[4,1568,64]{2,1,0:T(8,128)(2,1)S(1)}, bf16[4,1568,64]{2,1,0:T(8,128)(2,1)S(1)}, bf16[4,1568,64]{2,1,0:T(8,128)(2,1)}, /*index=5*/s32[]{:T(128)}) while((s32[]{:T(128)}, bf16[4,1568,64]{1,2,0:T(8,128)(2,1)}, bf16[4,1568,64]{2,1,0:T(8,128)(2,1)S(1)}, ...), condition=%wide.region_5.6_spmd, body=%wide.region_2.5_spmd.sunk | while | flops 651632576 | bytes 30954188 | solution.py:117
  698.1 34.1 %all-to-all-done.3 = bf16[4,2,50176]{2,1,0:T(2,128)(2,1)S(1)} async-done(((bf16[4,2,50176]{2,1,0:T(2,128)(2,1)}), bf16[4,2,50176]{2,1,0:T(2,128)(2,1)S(1)}, u32[]{:S(2)}, u32[]{:S(2)}) %all-to-all-start.3) | async-done | bytes 802848 | tf_op jit(solution)/shard_map/all_to_all | solution.py:118
  739.5 26.3 %fusion.137 = bf16[1,392,1024]{2,1,0:T(8,128)(2,1)} fusion(f32[392,1024]{1,0:T(8,128)S(1)} %get-tuple-element.220, bf16[4096,1024]{1,0:T(8,128)(2,1)} %all-gather.17.cloned.1.call-done, bf16[1024,4096]{1,0:T(8,128)(2,1)} %all-gather.15.cloned.1.call-done, f32[4096]{0:T(1024)S(1)} %copy-done.16, f32[]{:T(128)} %bitcast.42, f32[1024]{0:T(1024)S(1)} %copy-done.43, ...), kind=kOutput, calls=%fused_computation.190 | convolution fusion | flops 6686253056 | bytes 19217476 | tf_op jit(solution)/shard_map/dot_general | solution.py:128
  777.3 38.4 %all-reduce.9 = (f32[1024]{0:T(1024)S(1)}, f32[1024]{0:T(1024)S(1)}, f32[1024]{0:T(1024)S(1)}, f32[1024]{0:T(1024)S(1)}, f32[1024]{0:T(1024)S(1)}, /*index=5*/f3...) all-reduce(f32[1024]{0:T(1024)S(1)} %get-tuple-element.152, ...), channel_id=2, replica_groups=mesh['fsdp'=8,'seq'=4] {'fsdp','seq'}, use_global_device_ids=true, to_apply=%region_22.23.clone | all-reduce | flops 12288 | bytes 98304
  824.1 134.6 %reduce-scatter.11.cloned.1.call-done = f32[32,1024]{1,0:T(8,128)} async-done(((f32[1024,1024]{1,0:T(8,128)}), f32[32,1024]{1,0:T(8,128)}) %reduce-scatter.11.cloned.1.call-update) | async-done | bytes 131088 | tf_op jit(solution)/shard_map/reduce_scatter | solution.py:287
  958.6 365.9 %reduce-scatter.15.cloned.1.call-done = f32[32,4096]{1,0:T(8,128)} async-done(((f32[1024,4096]{1,0:T(8,128)}), f32[32,4096]{1,0:T(8,128)}) %reduce-scatter.15.cloned.1.call-update) | async-done | bytes 524304 | tf_op jit(solution)/shard_map/reduce_scatter | solution.py:293
  1324.6 364.9 %reduce-scatter.17.cloned.1.call-done = f32[128,1024]{1,0:T(8,128)} async-done(((f32[4096,1024]{1,0:T(8,128)}), f32[128,1024]{1,0:T(8,128)}) %reduce-scatter.17.cloned.1.call-update) | async-done | bytes 524304 | tf_op jit(solution)/shard_map/reduce_scatter | solution.py:295
  (300 shorter events, 392.5 us)
Async XLA Ops:
  7.2 33.4 %all-gather.7.cloned.1.call-start = ((), (), s32[]{:S(2)}) async-start(), calls=%async_computation.14 | async-start | bytes 2359296 | tf_op jit(solution)/shard_map/all_gather | solution.py:172
  7.9 62.4 %all-gather.9.cloned.1.call-start = ((), (), s32[]{:S(2)}) async-start(), calls=%async_computation.15 | async-start | bytes 2359296 | tf_op jit(solution)/shard_map/all_gather | solution.py:173
  8.7 91.5 %all-gather.11.cloned.1.call-start = ((), (), s32[]{:S(2)}) async-start(), calls=%async_computation.16 | async-start | bytes 2359296 | tf_op jit(solution)/shard_map/all_gather | solution.py:174
  9.4 201.3 %all-gather.13.cloned.1.call-start = ((), (), s32[]{:S(2)}) async-start(), calls=%async_computation.17 | async-start | bytes 2359296 | tf_op jit(solution)/shard_map/all_gather | solution.py:175
  10.0 205.5 %all-gather.15.cloned.1.call-start = ((), (), s32[]{:S(2)}) async-start(), calls=%async_computation.18 | async-start | bytes 9437184 | tf_op jit(solution)/shard_map/all_gather | solution.py:178
  11.9 88.3 %copy-start.17 = (f32[392]{0:T(512)}, f32[392]{0:T(512)S(1)}, u32[]{:S(2)}) copy-start(f32[392]{0:T(512)S(1)} %broadcast_multiply_fusion.6) | copy-start | bytes 4708
  13.4 86.8 %copy-start.24 = (f32[392]{0:T(512)}, f32[392]{0:T(512)S(1)}, u32[]{:S(2)}) copy-start(f32[392]{0:T(512)S(1)} %add_rsqrt_fusion.2) | copy-start | bytes 4708
  13.4 56.9 %copy-start.2 = (bf16[1,392,1024]{2,1,0:T(8,128)(2,1)S(1)}, bf16[1,392,1024]{2,1,0:T(8,128)(2,1)}, u32[]{:S(2)}) copy-start(bf16[1,392,1024]{2,1,0:T(8,128)(2,1)} %param.24) | copy-start | bytes 2408452
  13.4 56.9 %copy-start.29 = (f32[1024]{0:T(1024)S(1)}, f32[1024]{0:T(1024)}, u32[]{:S(2)}) copy-start(f32[1024]{0:T(1024)} %param.26) | copy-start | bytes 12292
  44.8 30.8 %all-to-all-start = ((bf16[1,392,16,64]{1,3,0,2:T(8,128)(2,1)}), bf16[1,392,16,64]{1,3,0,2:T(8,128)(2,1)S(1)}, u32[]{:S(2)}, u32[]{:S(2)}) async-start(bf16[1,392,16,64]{1,3,0,2:T(8,128)(2,1)} %bitcast.17), calls=%async_computation | async-start | bytes 2097152 | tf_op jit(solution)/shard_map/all_to_all | solution.py:110
  75.6 29.7 %all-to-all-start.1 = ((bf16[1,392,16,64]{1,3,0,2:T(8,128)(2,1)}), bf16[1,392,16,64]{1,3,0,2:T(8,128)(2,1)}, u32[]{:S(2)}, u32[]{:S(2)}) async-start(bf16[1,392,16,64]{1,3,0,2:T(8,128)(2,1)} %bitcast.24), calls=%async_computation.1 | async-start | bytes 2097152 | tf_op jit(solution)/shard_map/all_to_all | solution.py:111
  105.4 29.8 %all-to-all-start.2 = ((bf16[1,392,16,64]{1,3,0,2:T(8,128)(2,1)}), bf16[1,392,16,64]{1,3,0,2:T(8,128)(2,1)}, u32[]{:S(2)}, u32[]{:S(2)}) async-start(bf16[1,392,16,64]{1,3,0,2:T(8,128)(2,1)} %bitcast.31), calls=%async_computation.2 | async-start | bytes 2097152 | tf_op jit(solution)/shard_map/all_to_all | solution.py:112
  109.6 132.6 %all-gather.17.cloned.1.call-start = ((), (), s32[]{:S(2)}) async-start(), calls=%async_computation.19 | async-start | bytes 9437184 | tf_op jit(solution)/shard_map/all_gather | solution.py:179
  178.5 24.3 %all-to-all-start.4 = ((bf16[4,2,50176]{2,1,0:T(2,128)(2,1)}), bf16[4,2,50176]{2,1,0:T(2,128)(2,1)}, u32[]{:S(2)}, u32[]{:S(2)}) async-start(bf16[4,2,50176]{2,1,0:T(2,128)(2,1)} %reshape.363), calls=%async_computation.4 | async-start | bytes 1605632 | tf_op jit(solution)/shard_map/all_to_all | solution.py:118
  182.7 641.4 %reduce-scatter.13.cloned.1.call-start = ((), (), s32[]{:S(2)}) async-start(), calls=%async_computation.23 | async-start | bytes 4325376 | tf_op jit(solution)/shard_map/reduce_scatter | solution.py:289
  267.2 10.4 collective-permute-start.2
  270.5 31.7 %collective-permute-start.1 = (bf16[1,392,4,64]{1,3,2,0:T(8,128)(2,1)}, bf16[1,392,4,64]{1,3,2,0:T(8,128)(2,1)}, u32[]{:S(2)}, u32[]{:S(2)}) collective-permute-start(bf16[1,392,4,64]{1,3,2,0:T(8,128)(2,1)} %get-tuple-element.217), channel_id=1, source_target_pairs={{0,2},{1,3},{2,0},{3,1},{4,6},{5,7},{6,4},{7,5},{8,10},{9,11},{10,... | collective-permute-start | bytes 602120 | tf_op jit(solution)/shard_map/ppermute | solution.py:29
  270.5 31.7 %collective-permute-start = (bf16[1,392,4,64]{1,3,2,0:T(8,128)(2,1)}, bf16[1,392,4,64]{1,3,2,0:T(8,128)(2,1)}, u32[]{:S(2)}, u32[]{:S(2)}) collective-permute-start(bf16[1,392,4,64]{1,3,2,0:T(8,128)(2,1)} %get-tuple-element.218), channel_id=1, source_target_pairs={{0,1},{1,2},{2,3},{3,0},{4,5},{5,6},{6,7},{7,4},{8,9},{9,10},{10,1... | collective-permute-start | bytes 602120 | tf_op jit(solution)/shard_map/ppermute | solution.py:29
  276.6 547.5 %reduce-scatter.7.cloned.1.call-start = ((), (), s32[]{:S(2)}) async-start(), calls=%async_computation.20 | async-start | bytes 4325376 | tf_op jit(solution)/shard_map/reduce_scatter | solution.py:284
  496.9 327.2 %reduce-scatter.9.cloned.1.call-start = ((), (), s32[]{:S(2)}) async-start(), calls=%async_computation.21 | async-start | bytes 4325376 | tf_op jit(solution)/shard_map/reduce_scatter | solution.py:286
  561.9 396.7 %reduce-scatter.11.cloned.1.call-start = ((), (), s32[]{:S(2)}) async-start(), calls=%async_computation.22 | async-start | bytes 4325376 | tf_op jit(solution)/shard_map/reduce_scatter | solution.py:287
  625.7 698.9 %reduce-scatter.15.cloned.1.call-start = ((), (), s32[]{:S(2)}) async-start(), calls=%async_computation.24 | async-start | bytes 17301504 | tf_op jit(solution)/shard_map/reduce_scatter | solution.py:293
  639.4 1050.1 %reduce-scatter.17.cloned.1.call-start = ((), (), s32[]{:S(2)}) async-start(), calls=%async_computation.25 | async-start | bytes 17301504 | tf_op jit(solution)/shard_map/reduce_scatter | solution.py:295
  694.2 37.9 %all-to-all-start.3 = ((bf16[4,2,50176]{2,1,0:T(2,128)(2,1)}), bf16[4,2,50176]{2,1,0:T(2,128)(2,1)S(1)}, u32[]{:S(2)}, u32[]{:S(2)}) async-start(bf16[4,2,50176]{2,1,0:T(2,128)(2,1)} %reshape.361), calls=%async_computation.3 | async-start | bytes 1605632 | tf_op jit(solution)/shard_map/all_to_all | solution.py:118
  (50 other events, 679.4 us)
Sparse Core Ops, SparseCore 0:
  9.9 30.5 all-gather.6
  42.4 27.8 all-gather.8
  72.2 27.8 all-gather.10
  101.9 27.8 all-gather.12
  131.6 54.4 all-gather.14
  187.8 54.3 all-gather.16
  276.7 152.5 reduce-scatter.12
  497.0 155.7 reduce-scatter.6
  655.6 153.8 reduce-scatter.8
  812.2 146.4 reduce-scatter.10
  961.5 363.0 reduce-scatter.14
  1327.3 362.1 reduce-scatter.16
